TPU v7x, 256 devices: a whole 4x4x8 slice. The times are simulated.
256 devices in a mesh: cells: 16 (over z, core), lev: 16 (over x, y).
Axes of the slice: x: 4, y: 4, z: 8, core: 2. Of those that a mesh axis runs over, the one named last changes fastest.
Arguments:
- source_levels: float32 [128, 65536], P('lev', 'cells'), may hold values from -6 to 6
- level_to_mode: float32 [128, 128], replicated, may hold values from -0.5 to 0.5
- mode_to_level: float32 [128, 128], replicated, may hold values from -0.5 to 0.5
- mode_shift: float32 [128], P('lev'), may hold values from 0.02 to 1
- edge_weight: float32 [6, 65536], P(None, 'cells'), may hold values from 0.05 to 0.5
- neighbours: int32 [6, 65536], P(None, 'cells'), may hold values from 0 to 6143, as said below
- send_lists: int32 [16, 2048], P('cells'), may hold values from 0 to 4095, as said below
Outputs:
- correction: float32 [128, 65536], P('lev', 'cells')
Inputs may be any that keep to these rules, and one draw needn't show every extreme that they name: `neighbours`: an entry below 4096 is a cell of the same partition whose local index differs from the cell's own local index by at most 32; an entry e of partition p at or above 4096 names halo slot h = (e - 4096) % 128 from partition s = (e - 4096) // 128, with s not p and h below the number of cells that s sends to p. An unused entry names the cell itself. `send_lists`: the number of used slots from partition s to partition q differs from pair to pair: 1 to 128 for every pair of different partitions, 0 for a partition and itself; in every draw some partition receives 128 cells from every other one. Unused slots hold any cell.
All inputs are finite; a program needn't handle non-finite values.
Results may differ from a plain program's by a relative error of at most 0.00007.
Values sent between devices are 32-bit elements; how exact they have to be, the bound alone decides.
A program may use at most 64 MiB of HBM per device.

v0:
```python
import jax
import jax.numpy as jnp
from jax import lax
from jax.sharding import PartitionSpec as P

DEG = 6
HMAX = 128
SWEEPS = 2
STEPS = 4


def full_product(left, right):
    return jnp.dot(left, right, precision=lax.Precision.HIGHEST, preferred_element_type=jnp.float32)


def local(
    source_levels, level_to_mode, mode_to_level, mode_shift, edge_weight, neighbours, send_lists
):
    slab_rows = source_levels.shape[0]
    position = lax.axis_index("lev")
    send_cells = send_lists.reshape(-1)
    slot_total = send_cells.shape[0]
    diagonal = jnp.sum(edge_weight, axis=0)
    own_rows = lax.dynamic_slice_in_dim(level_to_mode, position * slab_rows, slab_rows, 0)
    mode_field = full_product(own_rows, lax.all_gather(source_levels, "lev", axis=0, tiled=True))
    shift_col = mode_shift[:, None]
    own_scale = shift_col + diagonal[None, :]

    def apply_operator(field):
        outgoing = jnp.take(field, send_cells, axis=1)
        arrived = lax.all_to_all(
            outgoing.reshape(slab_rows, -1, HMAX), "cells", split_axis=1, concat_axis=1, tiled=True
        ).reshape(slab_rows, slot_total)
        extended = jnp.concatenate([field, arrived], axis=1)
        running = own_scale * field
        for slot_number in range(DEG):
            running = running - edge_weight[slot_number][None, :] * jnp.take(
                extended, neighbours[slot_number], axis=1
            )
        return running

    radius = DEG / 2.0
    centre = shift_col + radius
    sigma_ratio = centre / radius
    answer = jnp.zeros_like(mode_field)
    remain = mode_field
    direction = jnp.zeros_like(mode_field)
    factor = 1.0 / sigma_ratio
    for sweep_index in range(SWEEPS):
        for step_index in range(STEPS):
            if step_index == 0:
                if sweep_index > 0:
                    remain = remain - apply_operator(direction)
                factor = 1.0 / sigma_ratio
                direction = remain / centre
            else:
                remain = remain - apply_operator(direction)
                newer = 1.0 / (2.0 * sigma_ratio - factor)
                direction = newer * factor * direction + 2.0 * newer / radius * remain
                factor = newer
            answer = answer + direction
    own_columns = lax.dynamic_slice_in_dim(mode_to_level, position * slab_rows, slab_rows, 1)
    return lax.psum_scatter(
        full_product(own_columns, answer), "lev", scatter_dimension=0, tiled=True
    )


def solution(mesh):
    in_specs = (
        P("lev", "cells"),
        P(),
        P(),
        P("lev"),
        P(None, "cells"),
        P(None, "cells"),
        P("cells", None),
    )
    out_specs = P("lev", "cells")
    return jax.shard_map(local, mesh=mesh, in_specs=in_specs, out_specs=out_specs, check_vma=False)
```

profile of v0, /device:TPU:1, one launch (start us, length us, event | category | flops | bytes accessed | tf_op | source)
XLA Modules:
  0.0 1055.3 jit_solution(7952593365196662498)
XLA Ops:
  21.0 41.8 %all-gather.2.cloned.1.call-done = f32[128,4096]{1,0:T(8,128)} async-done(((f32[8,4096]{1,0:T(8,128)}), f32[128,4096]{1,0:T(8,128)}) %all-gather.2.cloned.1.call-update) | async-done | bytes 2097168 | tf_op jit(solution)/shard_map/all_gather | solution.py:25
  93.4 15.4 %gather_fusion.6 = f32[4096,8]{1,0:T(8,128)} fusion(f32[8,6144]{0,1:T(8,128)S(1)} %copy.108, s32[4096]{0:T(1024)} %fusion.90), kind=kCustom, calls=%fused_computation.12.clone | custom fusion | bytes 278528 | tf_op jit(solution)/shard_map/jit(_take)/gather | solution.py:37
  337.2 15.4 %gather_fusion.20 = f32[4096,8]{1,0:T(8,128)} fusion(f32[8,6144]{0,1:T(8,128)S(1)} %copy.136, s32[4096]{0:T(1024)} %fusion.90), kind=kCustom, calls=%fused_computation.24.clone | custom fusion | bytes 278528 | tf_op jit(solution)/shard_map/jit(_take)/gather | solution.py:37
  352.6 15.4 %gather_fusion.19 = f32[4096,8]{1,0:T(8,128)} fusion(f32[8,6144]{0,1:T(8,128)S(1)} %copy.136, s32[4096]{0:T(1024)} %fusion.89), kind=kCustom, calls=%fused_computation.23.clone | custom fusion | bytes 278528 | tf_op jit(solution)/shard_map/jit(_take)/gather | solution.py:37
  368.0 15.4 %gather_fusion.18 = f32[4096,8]{1,0:T(8,128)} fusion(f32[8,6144]{0,1:T(8,128)S(1)} %copy.136, s32[4096]{0:T(1024)} %fusion.88), kind=kCustom, calls=%fused_computation.22.clone | custom fusion | bytes 278528 | tf_op jit(solution)/shard_map/jit(_take)/gather | solution.py:37
  398.9 15.4 %gather_fusion.16 = f32[4096,8]{1,0:T(8,128)} fusion(f32[8,6144]{0,1:T(8,128)S(1)} %copy.136, s32[4096]{0:T(1024)} %fusion.86), kind=kCustom, calls=%fused_computation.20.clone | custom fusion | bytes 278528 | tf_op jit(solution)/shard_map/jit(_take)/gather | solution.py:37
  414.3 15.4 %gather_fusion.15 = f32[4096,8]{1,0:T(8,128)} fusion(f32[8,6144]{0,1:T(8,128)S(1)} %copy.136, s32[4096]{0:T(1024)} %fusion.85), kind=kCustom, calls=%fused_computation.19.clone | custom fusion | bytes 278528 | tf_op jit(solution)/shard_map/jit(_take)/gather | solution.py:37
  465.5 15.4 %gather_fusion.27 = f32[4096,8]{1,0:T(8,128)} fusion(f32[8,6144]{0,1:T(8,128)S(1)} %copy.150, s32[4096]{0:T(1024)} %fusion.90), kind=kCustom, calls=%fused_computation.30.clone | custom fusion | bytes 278528 | tf_op jit(solution)/shard_map/jit(_take)/gather | solution.py:37
  496.3 15.4 %gather_fusion.25 = f32[4096,8]{1,0:T(8,128)} fusion(f32[8,6144]{0,1:T(8,128)S(1)} %copy.150, s32[4096]{0:T(1024)} %fusion.88), kind=kCustom, calls=%fused_computation.28.clone | custom fusion | bytes 278528 | tf_op jit(solution)/shard_map/jit(_take)/gather | solution.py:37
  527.1 15.4 %gather_fusion.23 = f32[4096,8]{1,0:T(8,128)} fusion(f32[8,6144]{0,1:T(8,128)S(1)} %copy.150, s32[4096]{0:T(1024)} %fusion.86), kind=kCustom, calls=%fused_computation.26.clone | custom fusion | bytes 278528 | tf_op jit(solution)/shard_map/jit(_take)/gather | solution.py:37
  542.6 15.4 %gather_fusion.22 = f32[4096,8]{1,0:T(8,128)} fusion(f32[8,6144]{0,1:T(8,128)S(1)} %copy.150, s32[4096]{0:T(1024)} %fusion.85), kind=kCustom, calls=%fused_computation.25.clone | custom fusion | bytes 278528 | tf_op jit(solution)/shard_map/jit(_take)/gather | solution.py:37
  592.7 15.4 %gather_fusion.34 = f32[4096,8]{1,0:T(8,128)} fusion(f32[8,6144]{0,1:T(8,128)S(1)} %copy.164, s32[4096]{0:T(1024)} %fusion.90), kind=kCustom, calls=%fused_computation.36.clone | custom fusion | bytes 278528 | tf_op jit(solution)/shard_map/jit(_take)/gather | solution.py:37
  623.6 15.4 %gather_fusion.32 = f32[4096,8]{1,0:T(8,128)} fusion(f32[8,6144]{0,1:T(8,128)S(1)} %copy.164, s32[4096]{0:T(1024)} %fusion.88), kind=kCustom, calls=%fused_computation.34.clone | custom fusion | bytes 278528 | tf_op jit(solution)/shard_map/jit(_take)/gather | solution.py:37
  654.4 15.4 %gather_fusion.30 = f32[4096,8]{1,0:T(8,128)} fusion(f32[8,6144]{0,1:T(8,128)S(1)} %copy.164, s32[4096]{0:T(1024)} %fusion.86), kind=kCustom, calls=%fused_computation.32.clone | custom fusion | bytes 278528 | tf_op jit(solution)/shard_map/jit(_take)/gather | solution.py:37
  669.8 15.4 %gather_fusion.29 = f32[4096,8]{1,0:T(8,128)} fusion(f32[8,6144]{0,1:T(8,128)S(1)} %copy.164, s32[4096]{0:T(1024)} %fusion.85), kind=kCustom, calls=%fused_computation.31.clone | custom fusion | bytes 278528 | tf_op jit(solution)/shard_map/jit(_take)/gather | solution.py:37
  719.4 15.4 %gather_fusion.41 = f32[4096,8]{1,0:T(8,128)} fusion(f32[8,6144]{0,1:T(8,128)S(1)} %copy.178, s32[4096]{0:T(1024)} %fusion.90), kind=kCustom, calls=%fused_computation.42.clone | custom fusion | bytes 278528 | tf_op jit(solution)/shard_map/jit(_take)/gather | solution.py:37
  750.2 15.4 %gather_fusion.39 = f32[4096,8]{1,0:T(8,128)} fusion(f32[8,6144]{0,1:T(8,128)S(1)} %copy.178, s32[4096]{0:T(1024)} %fusion.88), kind=kCustom, calls=%fused_computation.40.clone | custom fusion | bytes 278528 | tf_op jit(solution)/shard_map/jit(_take)/gather | solution.py:37
  781.1 15.4 %gather_fusion.37 = f32[4096,8]{1,0:T(8,128)} fusion(f32[8,6144]{0,1:T(8,128)S(1)} %copy.178, s32[4096]{0:T(1024)} %fusion.86), kind=kCustom, calls=%fused_computation.38.clone | custom fusion | bytes 278528 | tf_op jit(solution)/shard_map/jit(_take)/gather | solution.py:37
  796.5 15.4 %gather_fusion.36 = f32[4096,8]{1,0:T(8,128)} fusion(f32[8,6144]{0,1:T(8,128)S(1)} %copy.178, s32[4096]{0:T(1024)} %fusion.85), kind=kCustom, calls=%fused_computation.37.clone | custom fusion | bytes 278528 | tf_op jit(solution)/shard_map/jit(_take)/gather | solution.py:37
  846.7 15.4 %gather_fusion.48 = f32[4096,8]{1,0:T(8,128)} fusion(f32[8,6144]{0,1:T(8,128)S(1)} %copy.192, s32[4096]{0:T(1024)} %fusion.90), kind=kCustom, calls=%fused_computation.48.clone | custom fusion | bytes 278528 | tf_op jit(solution)/shard_map/jit(_take)/gather | solution.py:37
  877.6 15.4 %gather_fusion.46 = f32[4096,8]{1,0:T(8,128)} fusion(f32[8,6144]{0,1:T(8,128)S(1)} %copy.192, s32[4096]{0:T(1024)} %fusion.88), kind=kCustom, calls=%fused_computation.46.clone | custom fusion | bytes 278528 | tf_op jit(solution)/shard_map/jit(_take)/gather | solution.py:37
  908.4 15.4 %gather_fusion.44 = f32[4096,8]{1,0:T(8,128)} fusion(f32[8,6144]{0,1:T(8,128)S(1)} %copy.192, s32[4096]{0:T(1024)} %fusion.86), kind=kCustom, calls=%fused_computation.44.clone | custom fusion | bytes 278528 | tf_op jit(solution)/shard_map/jit(_take)/gather | solution.py:37
  923.8 15.4 %gather_fusion.43 = f32[4096,8]{1,0:T(8,128)} fusion(f32[8,6144]{0,1:T(8,128)S(1)} %copy.192, s32[4096]{0:T(1024)} %fusion.85), kind=kCustom, calls=%fused_computation.43.clone | custom fusion | bytes 278528 | tf_op jit(solution)/shard_map/jit(_take)/gather | solution.py:37
  954.5 92.4 %all-reduce.3.cloned.1.call-done = f32[128,4096]{1,0:T(8,128)} async-done(((f32[128,4096]{1,0:T(8,128)}), f32[128,4096]{1,0:T(8,128)}) %all-reduce.3.cloned.1.call-update) | async-done | bytes 2097168
  (422 shorter events, 566.0 us)
Async XLA Ops:
  6.5 943.2 %copy-start = (f32[128,128]{1,0:T(8,128)S(1)}, f32[128,128]{1,0:T(8,128)}, u32[]{:S(2)}) copy-start(f32[128,128]{1,0:T(8,128)} %param.13) | copy-start | bytes 196612
  6.5 56.2 %all-gather.2.cloned.1.call-start = ((), (), s32[]{:S(2)}) async-start(), calls=%async_computation.7 | async-start | bytes 2228224 | tf_op jit(solution)/shard_map/all_gather | solution.py:25
  11.1 54.3 %copy-start.115 = (f32[8]{0:T(128)}, f32[8]{0:T(128)S(1)}, u32[]{:S(2)}) copy-start(f32[8]{0:T(128)S(1)} %get-tuple-element.40) | copy-start | bytes 100
  65.4 130.4 %copy-start.19 = (f32[8,4096]{1,0:T(8,128)}, f32[8,4096]{1,0:T(8,128)S(1)}, u32[]{:S(2)}) copy-start(f32[8,4096]{1,0:T(8,128)S(1)} %get-tuple-element.42) | copy-start | bytes 393220
  72.5 10.5 copy-start.134
  72.5 10.5 copy-start.135
  74.5 16.3 %all-to-all-start = ((f32[8,16,128]{2,0,1:T(8,128)}), f32[8,16,128]{2,0,1:T(8,128)S(1)}, u32[]{:S(2)}, u32[]{:S(2)}) async-start(f32[8,16,128]{2,0,1:T(8,128)} %copy.107), calls=%async_computation | async-start | bytes 131072 | tf_op jit(solution)/shard_map/all_to_all | solution.py:31
  93.4 18.3 %copy-start.49 = (s32[4096]{0:T(1024)S(1)}, s32[4096]{0:T(1024)}, u32[]{:S(2)}) copy-start(s32[4096]{0:T(1024)} %fusion.89) | copy-start | bytes 49156
  111.6 16.9 %copy-start.47 = (s32[4096]{0:T(1024)S(1)}, s32[4096]{0:T(1024)}, u32[]{:S(2)}) copy-start(s32[4096]{0:T(1024)} %fusion.88) | copy-start | bytes 49156
  128.5 16.9 %copy-start.45 = (s32[4096]{0:T(1024)S(1)}, s32[4096]{0:T(1024)}, u32[]{:S(2)}) copy-start(s32[4096]{0:T(1024)} %fusion.87) | copy-start | bytes 49156
  145.4 16.9 %copy-start.41 = (s32[4096]{0:T(1024)S(1)}, s32[4096]{0:T(1024)}, u32[]{:S(2)}) copy-start(s32[4096]{0:T(1024)} %fusion.86) | copy-start | bytes 49156
  162.4 16.9 %copy-start.43 = (s32[4096]{0:T(1024)S(1)}, s32[4096]{0:T(1024)}, u32[]{:S(2)}) copy-start(s32[4096]{0:T(1024)} %fusion.85) | copy-start | bytes 49156
  205.3 13.1 %copy-start.51 = (s32[4096]{0:T(1024)S(1)}, s32[4096]{0:T(1024)}, u32[]{:S(2)}) copy-start(s32[4096]{0:T(1024)} %fusion.90) | copy-start | bytes 49156
  216.5 16.0 %copy-start.50 = (s32[4096]{0:T(1024)S(1)}, s32[4096]{0:T(1024)}, u32[]{:S(2)}) copy-start(s32[4096]{0:T(1024)} %fusion.89) | copy-start | bytes 49156
  216.5 30.1 %copy-start.48 = (s32[4096]{0:T(1024)S(1)}, s32[4096]{0:T(1024)}, u32[]{:S(2)}) copy-start(s32[4096]{0:T(1024)} %fusion.88) | copy-start | bytes 49156
  218.4 42.4 %copy-start.46 = (s32[4096]{0:T(1024)S(1)}, s32[4096]{0:T(1024)}, u32[]{:S(2)}) copy-start(s32[4096]{0:T(1024)} %fusion.87) | copy-start | bytes 49156
  218.4 56.4 %copy-start.42 = (s32[4096]{0:T(1024)S(1)}, s32[4096]{0:T(1024)}, u32[]{:S(2)}) copy-start(s32[4096]{0:T(1024)} %fusion.86) | copy-start | bytes 49156
  232.5 56.4 %copy-start.44 = (s32[4096]{0:T(1024)S(1)}, s32[4096]{0:T(1024)}, u32[]{:S(2)}) copy-start(s32[4096]{0:T(1024)} %fusion.85) | copy-start | bytes 49156
  323.2 11.4 %all-to-all-start.2 = ((f32[8,16,128]{2,0,1:T(8,128)}), f32[8,16,128]{2,0,1:T(8,128)S(1)}, u32[]{:S(2)}, u32[]{:S(2)}) async-start(f32[8,16,128]{2,0,1:T(8,128)} %copy.135), calls=%async_computation.2 | async-start | bytes 131072 | tf_op jit(solution)/shard_map/all_to_all | solution.py:31
  326.8 720.1 %all-reduce.3.cloned.1.call-start = ((), (), s32[]{:S(2)}) async-start(), calls=%async_computation.8 | async-start | bytes 4194304
  442.5 20.4 %copy-start.1 = (f32[8,4096]{1,0:T(8,128)}, f32[8,4096]{1,0:T(8,128)S(1)}, u32[]{:S(2)}) copy-start(f32[8,4096]{1,0:T(8,128)S(1)} %get-tuple-element.13) | copy-start | bytes 393220
  578.5 11.7 %copy-start.26 = (f32[8,4096]{1,0:T(8,128)S(1)}, f32[8,4096]{1,0:T(8,128)}, u32[]{:S(2)}) copy-start(f32[8,4096]{1,0:T(8,128)} %copy-done.25) | copy-start | bytes 393220
  696.5 20.4 %copy-start.4 = (f32[8,4096]{1,0:T(8,128)}, f32[8,4096]{1,0:T(8,128)S(1)}, u32[]{:S(2)}) copy-start(f32[8,4096]{1,0:T(8,128)S(1)} %get-tuple-element.9) | copy-start | bytes 393220
  832.4 11.8 %copy-start.24 = (f32[8,4096]{1,0:T(8,128)S(1)}, f32[8,4096]{1,0:T(8,128)}, u32[]{:S(2)}) copy-start(f32[8,4096]{1,0:T(8,128)} %copy-done.23) | copy-start | bytes 393220
  (119 other events, 431.7 us)
Sparse Core Ops, SparseCore 0:
  9.8 52.8 all-gather.1
  953.3 93.5 all-reduce.2
where the time goes:
time: 1070 us; the launch traced here: 1060 us
  local copies, waits for them, and re-layouts  788 us (74%)
  waiting for transfers between devices  149 us (14%)
  blocking collectives  52 us (5%)
  other arithmetic  32.2 us (3%)
  between operations  15.8 us (1%)
  starting transfers between devices  12.2 us (1%)
    gather x84, local copies, waits for them, and re-layouts, apply_operator(): jnp.take(extended, neighbours[slot_number], axis=1)  712 us
    unnamed x3, waiting for transfers between devices  93.1 us
    all_to_all x5, blocking collectives, apply_operator(): lax.all_to_all(outgoing.reshape(slab_rows, -1, HMAX), 'cells', split_axis...  52 us
    gather x7, local copies, waits for them, and re-layouts, apply_operator(): outgoing = jnp.take(field, send_cells, axis=1)  47.4 us
    all_gather x1, waiting for transfers between devices, local(): lax.all_gather(source_levels, 'lev', axis=0, tiled=True)  41.8 us
  transfers between devices with their start and end apart: 4, of which 4 were waited for; matrix products, arithmetic and copies ran while one was open for 1% of the time, Pallas kernels for 0%

commit v1 on v0

--- a/solution.py
+++ b/solution.py
@@ -7,6 +7,28 @@
 HMAX = 128
 SWEEPS = 2
 STEPS = 4
+
+
+def joined_along(tiles, dim):
+    tiles = jnp.moveaxis(tiles, 0, dim)
+    shape = tiles.shape
+    return tiles.reshape(*shape[:dim], shape[dim] * shape[dim + 1], *shape[dim + 2 :])
+
+
+def gather_around(array, axis, dim):
+    length = lax.axis_size(axis)
+    pairs = [(i, (i + 1) % length) for i in range(length)]
+    back = [(b, a) for a, b in pairs]
+    lower, upper = ([], [])
+    for hop in range(length - 1):
+        if hop % 2 == 0:
+            lower.append(lax.ppermute(lower[-1] if lower else array, axis, pairs))
+        else:
+            upper.append(lax.ppermute(upper[-1] if upper else array, axis, back))
+    tiles = jnp.stack([*lower[::-1], array, *upper])
+    shift = lax.axis_index(axis) - len(lower)
+    tiles = tiles[(jnp.arange(length) - shift) % length]
+    return joined_along(tiles, dim)
 
 
 def full_product(left, right):
@@ -22,7 +44,7 @@
     slot_total = send_cells.shape[0]
     diagonal = jnp.sum(edge_weight, axis=0)
     own_rows = lax.dynamic_slice_in_dim(level_to_mode, position * slab_rows, slab_rows, 0)
-    mode_field = full_product(own_rows, lax.all_gather(source_levels, "lev", axis=0, tiled=True))
+    mode_field = full_product(own_rows, gather_around(source_levels, "lev", 0))
     shift_col = mode_shift[:, None]
     own_scale = shift_col + diagonal[None, :]
 

time: 1070 us -> 1100 us (1.028)
  starting transfers between devices: 12.2 us -> 52.7 us
  waiting for transfers between devices: 149 us -> 112 us
  blocking collectives: 52 us -> 63.2 us
  local copies, waits for them, and re-layouts: 788 us -> 799 us
    all_gather x1 -> x0, waiting for transfers between devices: 41.8 us -> none  [local(): lax.all_gather(source_levels, 'lev', axis=0, tiled=True)]
    ppermute x0 -> x15, starting transfers between devices: none -> 35.3 us  [the longest x7 33.1 us: gather_around(): upper.append(lax.ppermute(upper[-1] if upper else array, axis, back))]
    ppermute x0 -> x15, waiting for transfers between devices: none -> 15.1 us  [the longest x8 15.1 us: gather_around(): lower.append(lax.ppermute(lower[-1] if lower else array, axis, pairs))]
    all_to_all x5 -> x6, blocking collectives: 52 us -> 63.2 us  [apply_operator(): lax.all_to_all(outgoing.reshape(slab_rows, -1, HMAX), 'cells', split_axis...]
    unnamed x3 -> x2, waiting for transfers between devices: 93.1 us -> 89.5 us
  transfers between devices with their start and end apart: 4 -> 17, of which waited for: 4 -> 9; matrix products, arithmetic and copies ran while one was open for 1% -> 2% of each run, Pallas kernels for 0% -> 0%
where the time goes in v1:
time: 1100 us; the launch traced here: 1080 us
  local copies, waits for them, and re-layouts  799 us (73%)
  waiting for transfers between devices  112 us (10%)
  blocking collectives  63.2 us (6%)
  starting transfers between devices  52.7 us (5%)
  other arithmetic  31.2 us (3%)
  between operations  16.2 us (1%)
    gather x84, local copies, waits for them, and re-layouts, apply_operator(): jnp.take(extended, neighbours[slot_number], axis=1)  712 us
    unnamed x2, waiting for transfers between devices  89.5 us
    all_to_all x6, blocking collectives, apply_operator(): lax.all_to_all(outgoing.reshape(slab_rows, -1, HMAX), 'cells', split_axis...  63.2 us
    gather x7, local copies, waits for them, and re-layouts, apply_operator(): outgoing = jnp.take(field, send_cells, axis=1)  46.4 us
    ppermute x7, starting transfers between devices, gather_around(): upper.append(lax.ppermute(upper[-1] if upper else array, axis, back))  33.1 us
  transfers between devices with their start and end apart: 17, of which 9 were waited for; matrix products, arithmetic and copies ran while one was open for 2% of the time, Pallas kernels for 0%

profile of v1, /device:TPU:1, one launch (start us, length us, event | category | flops | bytes accessed | tf_op | source)
XLA Modules:
  0.0 1078.7 jit_solution(5927287248831798010)
XLA Ops:
  93.0 17.4 %all-to-all-start = ((f32[8,16,128]{2,0,1:T(8,128)}), f32[8,16,128]{2,0,1:T(8,128)S(1)}, u32[]{:S(2)}, u32[]{:S(2)}) async-start(f32[8,16,128]{2,0,1:T(8,128)} %copy.107), calls=%async_computation | async-start | bytes 131072 | tf_op jit(solution)/shard_map/all_to_all | solution.py:53
  120.8 15.4 %gather_fusion.7 = f32[4096,8]{1,0:T(8,128)} fusion(f32[8,6144]{0,1:T(8,128)S(1)} %copy.108, s32[4096]{0:T(1024)} %get-tuple-element.49), kind=kCustom, calls=%fused_computation.12.clone | custom fusion | bytes 278528 | tf_op jit(solution)/shard_map/jit(_take)/gather | solution.py:59
  362.4 15.4 %gather_fusion.21 = f32[4096,8]{1,0:T(8,128)} fusion(f32[8,6144]{0,1:T(8,128)S(1)} %copy.136, s32[4096]{0:T(1024)} %get-tuple-element.49), kind=kCustom, calls=%fused_computation.24.clone | custom fusion | bytes 278528 | tf_op jit(solution)/shard_map/jit(_take)/gather | solution.py:59
  393.3 15.4 %gather_fusion.19 = f32[4096,8]{1,0:T(8,128)} fusion(f32[8,6144]{0,1:T(8,128)S(1)} %copy.136, s32[4096]{0:T(1024)} %get-tuple-element.47), kind=kCustom, calls=%fused_computation.22.clone | custom fusion | bytes 278528 | tf_op jit(solution)/shard_map/jit(_take)/gather | solution.py:59
  424.1 15.4 %gather_fusion.17 = f32[4096,8]{1,0:T(8,128)} fusion(f32[8,6144]{0,1:T(8,128)S(1)} %copy.136, s32[4096]{0:T(1024)} %get-tuple-element.45), kind=kCustom, calls=%fused_computation.20.clone | custom fusion | bytes 278528 | tf_op jit(solution)/shard_map/jit(_take)/gather | solution.py:59
  439.5 15.4 %gather_fusion.16 = f32[4096,8]{1,0:T(8,128)} fusion(f32[8,6144]{0,1:T(8,128)S(1)} %copy.136, s32[4096]{0:T(1024)} %get-tuple-element.44), kind=kCustom, calls=%fused_computation.19.clone | custom fusion | bytes 278528 | tf_op jit(solution)/shard_map/jit(_take)/gather | solution.py:59
  490.7 15.4 %gather_fusion.28 = f32[4096,8]{1,0:T(8,128)} fusion(f32[8,6144]{0,1:T(8,128)S(1)} %copy.150, s32[4096]{0:T(1024)} %get-tuple-element.49), kind=kCustom, calls=%fused_computation.30.clone | custom fusion | bytes 278528 | tf_op jit(solution)/shard_map/jit(_take)/gather | solution.py:59
  506.1 15.4 %gather_fusion.27 = f32[4096,8]{1,0:T(8,128)} fusion(f32[8,6144]{0,1:T(8,128)S(1)} %copy.150, s32[4096]{0:T(1024)} %get-tuple-element.48), kind=kCustom, calls=%fused_computation.29.clone | custom fusion | bytes 278528 | tf_op jit(solution)/shard_map/jit(_take)/gather | solution.py:59
  521.5 15.4 %gather_fusion.26 = f32[4096,8]{1,0:T(8,128)} fusion(f32[8,6144]{0,1:T(8,128)S(1)} %copy.150, s32[4096]{0:T(1024)} %get-tuple-element.47), kind=kCustom, calls=%fused_computation.28.clone | custom fusion | bytes 278528 | tf_op jit(solution)/shard_map/jit(_take)/gather | solution.py:59
  552.4 15.4 %gather_fusion.24 = f32[4096,8]{1,0:T(8,128)} fusion(f32[8,6144]{0,1:T(8,128)S(1)} %copy.150, s32[4096]{0:T(1024)} %get-tuple-element.45), kind=kCustom, calls=%fused_computation.26.clone | custom fusion | bytes 278528 | tf_op jit(solution)/shard_map/jit(_take)/gather | solution.py:59
  567.8 15.4 %gather_fusion.23 = f32[4096,8]{1,0:T(8,128)} fusion(f32[8,6144]{0,1:T(8,128)S(1)} %copy.150, s32[4096]{0:T(1024)} %get-tuple-element.44), kind=kCustom, calls=%fused_computation.25.clone | custom fusion | bytes 278528 | tf_op jit(solution)/shard_map/jit(_take)/gather | solution.py:59
  618.2 15.4 %gather_fusion.35 = f32[4096,8]{1,0:T(8,128)} fusion(f32[8,6144]{0,1:T(8,128)S(1)} %copy.164, s32[4096]{0:T(1024)} %get-tuple-element.49), kind=kCustom, calls=%fused_computation.36.clone | custom fusion | bytes 278528 | tf_op jit(solution)/shard_map/jit(_take)/gather | solution.py:59
  649.0 15.4 %gather_fusion.33 = f32[4096,8]{1,0:T(8,128)} fusion(f32[8,6144]{0,1:T(8,128)S(1)} %copy.164, s32[4096]{0:T(1024)} %get-tuple-element.47), kind=kCustom, calls=%fused_computation.34.clone | custom fusion | bytes 278528 | tf_op jit(solution)/shard_map/jit(_take)/gather | solution.py:59
  679.9 15.4 %gather_fusion.31 = f32[4096,8]{1,0:T(8,128)} fusion(f32[8,6144]{0,1:T(8,128)S(1)} %copy.164, s32[4096]{0:T(1024)} %get-tuple-element.45), kind=kCustom, calls=%fused_computation.32.clone | custom fusion | bytes 278528 | tf_op jit(solution)/shard_map/jit(_take)/gather | solution.py:59
  695.3 15.4 %gather_fusion.30 = f32[4096,8]{1,0:T(8,128)} fusion(f32[8,6144]{0,1:T(8,128)S(1)} %copy.164, s32[4096]{0:T(1024)} %get-tuple-element.44), kind=kCustom, calls=%fused_computation.31.clone | custom fusion | bytes 278528 | tf_op jit(solution)/shard_map/jit(_take)/gather | solution.py:59
  744.9 15.4 %gather_fusion.42 = f32[4096,8]{1,0:T(8,128)} fusion(f32[8,6144]{0,1:T(8,128)S(1)} %copy.178, s32[4096]{0:T(1024)} %get-tuple-element.49), kind=kCustom, calls=%fused_computation.42.clone | custom fusion | bytes 278528 | tf_op jit(solution)/shard_map/jit(_take)/gather | solution.py:59
  775.8 15.4 %gather_fusion.40 = f32[4096,8]{1,0:T(8,128)} fusion(f32[8,6144]{0,1:T(8,128)S(1)} %copy.178, s32[4096]{0:T(1024)} %get-tuple-element.47), kind=kCustom, calls=%fused_computation.40.clone | custom fusion | bytes 278528 | tf_op jit(solution)/shard_map/jit(_take)/gather | solution.py:59
  806.6 15.4 %gather_fusion.38 = f32[4096,8]{1,0:T(8,128)} fusion(f32[8,6144]{0,1:T(8,128)S(1)} %copy.178, s32[4096]{0:T(1024)} %get-tuple-element.45), kind=kCustom, calls=%fused_computation.38.clone | custom fusion | bytes 278528 | tf_op jit(solution)/shard_map/jit(_take)/gather | solution.py:59
  822.0 15.4 %gather_fusion.37 = f32[4096,8]{1,0:T(8,128)} fusion(f32[8,6144]{0,1:T(8,128)S(1)} %copy.178, s32[4096]{0:T(1024)} %get-tuple-element.44), kind=kCustom, calls=%fused_computation.37.clone | custom fusion | bytes 278528 | tf_op jit(solution)/shard_map/jit(_take)/gather | solution.py:59
  872.5 15.4 %gather_fusion.49 = f32[4096,8]{1,0:T(8,128)} fusion(f32[8,6144]{0,1:T(8,128)S(1)} %copy.192, s32[4096]{0:T(1024)} %get-tuple-element.49), kind=kCustom, calls=%fused_computation.48.clone | custom fusion | bytes 278528 | tf_op jit(solution)/shard_map/jit(_take)/gather | solution.py:59
  903.3 15.4 %gather_fusion.47 = f32[4096,8]{1,0:T(8,128)} fusion(f32[8,6144]{0,1:T(8,128)S(1)} %copy.192, s32[4096]{0:T(1024)} %get-tuple-element.47), kind=kCustom, calls=%fused_computation.46.clone | custom fusion | bytes 278528 | tf_op jit(solution)/shard_map/jit(_take)/gather | solution.py:59
  934.2 15.4 %gather_fusion.45 = f32[4096,8]{1,0:T(8,128)} fusion(f32[8,6144]{0,1:T(8,128)S(1)} %copy.192, s32[4096]{0:T(1024)} %get-tuple-element.45), kind=kCustom, calls=%fused_computation.44.clone | custom fusion | bytes 278528 | tf_op jit(solution)/shard_map/jit(_take)/gather | solution.py:59
  949.6 15.4 %gather_fusion.44 = f32[4096,8]{1,0:T(8,128)} fusion(f32[8,6144]{0,1:T(8,128)S(1)} %copy.192, s32[4096]{0:T(1024)} %get-tuple-element.44), kind=kCustom, calls=%fused_computation.43.clone | custom fusion | bytes 278528 | tf_op jit(solution)/shard_map/jit(_take)/gather | solution.py:59
  980.2 89.5 %all-reduce.3.cloned.1.call-done = f32[128,4096]{1,0:T(8,128)} async-done(((f32[128,4096]{1,0:T(8,128)}), f32[128,4096]{1,0:T(8,128)}) %all-reduce.3.cloned.1.call-update) | async-done | bytes 2097168
  (437 shorter events, 616.4 us)
Async XLA Ops:
  6.5 969.0 %copy-start = (f32[128,128]{1,0:T(8,128)S(1)}, f32[128,128]{1,0:T(8,128)}, u32[]{:S(2)}) copy-start(f32[128,128]{1,0:T(8,128)} %param.13) | copy-start | bytes 196612
  6.5 68.1 %copy-start.98 = (f32[8,4096]{1,0:T(8,128)S(1)}, f32[8,4096]{1,0:T(8,128)}, u32[]{:S(2)}) copy-start(f32[8,4096]{1,0:T(8,128)} %param.11) | copy-start | bytes 393220
  6.5 11.0 %collective-permute-start = (f32[8,4096]{1,0:T(8,128)}, f32[8,4096]{1,0:T(8,128)S(1)}, u32[]{:S(2)}, u32[]{:S(2)}) collective-permute-start(f32[8,4096]{1,0:T(8,128)} %param.11), channel_id=1, source_target_pairs={{0,1},{1,2},{2,3},{3,4},{4,5},{5,6},{6,7},{7,8},{8,9},{9,10},{10,1... | collective-permute-start | bytes 393224 | tf_op jit(solution)/shard_map/ppermute | solution.py:25
  8.7 16.6 %collective-permute-start.8 = (f32[8,4096]{1,0:T(8,128)}, f32[8,4096]{1,0:T(8,128)S(1)}, u32[]{:S(2)}, u32[]{:S(2)}) collective-permute-start(f32[8,4096]{1,0:T(8,128)} %param.11), channel_id=1, source_target_pairs={{1,0},{2,1},{3,2},{4,3},{5,4},{6,5},{7,6},{8,7},{9,8},{10,9},{11,1... | collective-permute-start | bytes 393224 | tf_op jit(solution)/shard_map/ppermute | solution.py:27
  17.6 7.1 collective-permute-start.1
  24.7 7.1 collective-permute-start.2
  25.3 7.1 collective-permute-start.9
  31.8 7.1 collective-permute-start.3
  32.5 7.8 collective-permute-start.10
  39.0 7.1 collective-permute-start.4
  40.3 7.1 collective-permute-start.11
  46.1 8.1 collective-permute-start.5
  47.4 8.1 collective-permute-start.12
  54.3 8.0 collective-permute-start.6
  55.5 26.7 %copy-start.105 = (f32[8]{0:T(128)}, f32[8]{0:T(128)S(1)}, u32[]{:S(2)}) copy-start(f32[8]{0:T(128)S(1)} %get-tuple-element.40) | copy-start | bytes 100
  55.5 8.3 collective-permute-start.13
  62.3 7.1 collective-permute-start.7
  63.8 15.4 %collective-permute-start.14 = (f32[8,4096]{1,0:T(8,128)S(1)}, f32[8,4096]{1,0:T(8,128)S(1)}, u32[]{:S(2)}, u32[]{:S(2)}) collective-permute-start(f32[8,4096]{1,0:T(8,128)S(1)} %collective-permute-done.13), channel_id=1, source_target_pairs={{1,0},{2,1},{3,2},{4,3},{5,4},{6,5},{7,6},{8,7},{9,8},{10,9},{11,1... | collective-permute-start | bytes 393224 | tf_op jit(solution)/shard_map/ppermute | solution.py:27
  84.0 139.1 %copy-start.19 = (f32[8,4096]{1,0:T(8,128)}, f32[8,4096]{1,0:T(8,128)S(1)}, u32[]{:S(2)}) copy-start(f32[8,4096]{1,0:T(8,128)S(1)} %get-tuple-element.42) | copy-start | bytes 393220
  91.1 19.4 %copy-start.121 = (f32[8]{0:T(128)S(1)}, f32[8]{0:T(128)}, u32[]{:S(2)}) copy-start(f32[8]{0:T(128)} %get-tuple-element.16) | copy-start | bytes 100
  93.0 25.2 %all-to-all-start = ((f32[8,16,128]{2,0,1:T(8,128)}), f32[8,16,128]{2,0,1:T(8,128)S(1)}, u32[]{:S(2)}, u32[]{:S(2)}) async-start(f32[8,16,128]{2,0,1:T(8,128)} %copy.107), calls=%async_computation | async-start | bytes 131072 | tf_op jit(solution)/shard_map/all_to_all | solution.py:53
  110.4 959.3 %all-reduce.3.cloned.1.call-start = ((), (), s32[]{:S(2)}) async-start(), calls=%async_computation.7 | async-start | bytes 4194304
  467.7 20.4 %copy-start.1 = (f32[8,4096]{1,0:T(8,128)}, f32[8,4096]{1,0:T(8,128)S(1)}, u32[]{:S(2)}) copy-start(f32[8,4096]{1,0:T(8,128)S(1)} %get-tuple-element.13) | copy-start | bytes 393220
  721.9 20.4 %copy-start.4 = (f32[8,4096]{1,0:T(8,128)}, f32[8,4096]{1,0:T(8,128)S(1)}, u32[]{:S(2)}) copy-start(f32[8,4096]{1,0:T(8,128)S(1)} %get-tuple-element.9) | copy-start | bytes 393220
  (119 other events, 626.8 us)
Sparse Core Ops, SparseCore 0:
  979.1 90.5 all-reduce.2
